TPU v7x, 128 devices: a whole 4x4x4 slice. The times are simulated.
128 devices in a mesh: req: 4 (over z_lo, core), seq: 32 (over y, x, z_hi).
Axes of the slice: x: 4, y: 4, z: 4 (z_hi: 2, z_lo: 2; z = z_hi * 2 + z_lo), core: 2. Of those that a mesh axis runs over, the one named last changes fastest.
Arguments:
- prefill_query: bfloat16 [16384, 1536], P(('req', 'seq')), may hold values from -512 to 512
- prefill_key: bfloat16 [16384, 512], P(('req', 'seq')), may hold values from -512 to 512
- prefill_value: bfloat16 [16384, 512], P(('req', 'seq')), may hold values from -6 to 6
- prefill_resid: bfloat16 [16384, 1536], P(('req', 'seq')), may hold values from -6 to 6
- dec_query: bfloat16 [16, 1536], P('req'), may hold values from -512 to 512
- dec_key_new: bfloat16 [16, 512], P('req'), may hold values from -16 to 16
- dec_value_new: bfloat16 [16, 512], P('req'), may hold values from -6 to 6
- dec_resid: bfloat16 [16, 1536], P('req'), may hold values from -6 to 6
- cache_lengths: int32 [16], P('req'), may hold values from 16 to 32768, as said below
- key_cache: bfloat16 [16, 32768, 512], P('req', 'seq'), may hold values from -512 to 512
- value_cache: bfloat16 [16, 32768, 512], P('req', 'seq'), may hold values from -6 to 6
- attn_out_weight: bfloat16 [1536, 1536], replicated, may hold values from -0.15625 to 0.15625
- ffn_gain: float32 [1536], replicated, may hold values from 0.1 to 1.9
- expert_gate: bfloat16 [32, 1536, 512], P('seq', 'req'), may hold values from -0.15625 to 0.15625
- expert_up: bfloat16 [32, 1536, 512], P('seq', 'req'), may hold values from -0.15625 to 0.15625
- expert_down: bfloat16 [32, 512, 1536], P('seq', None, 'req'), may hold values from -0.25 to 0.25
- routes: int32 [16384, 8], P(('req', 'seq')), may hold values from 0 to 31, all different within a row; in each aligned block of 128 rows (0 to 127, 128 to 255, ...) at most 40 rows name the same one
- route_weights: float32 [16384, 8], P(('req', 'seq')), may hold values from 0.05 to 0.5
Outputs:
- prefill_out: bfloat16 [16384, 1536], P(('req', 'seq'))
- dec_out: bfloat16 [16, 1536], P('req')
Inputs may be any that keep to these rules, and one draw needn't show every extreme that they name: `routes`: in each aligned block of 128 rows (the rows of one device) no expert is named by more than 40 rows. `cache_lengths`: some request uses all 32768 positions.
All inputs are finite; a program needn't handle non-finite values.
Results may differ from a plain program's by a relative error of at most 0.012.
Values may be sent and summed in bfloat16 or wider, within the bound.
No kernel may reach another device: no remote copies, remote signals or barrier semaphores. Data moves between devices by JAX's collectives and lax.ppermute only.
A program may use at most 128 MiB of HBM per device.

v0:
```python
import math
import jax
import jax.numpy as jnp
from jax import lax
from jax.sharding import PartitionSpec as P

D = 1536
HEADS = 24
KVH = 8
HD = 64
EXPERTS = 32
CAP = 40
NEGATIVE = -1e30
EPSILON = 1e-05


def rms_scale(hidden, gain):
    values_float = hidden.astype(jnp.float32)
    mean_square = jnp.mean(values_float * values_float, axis=-1, keepdims=True)
    return (values_float * lax.rsqrt(mean_square + EPSILON) * gain).astype(jnp.bfloat16)


def per_request(function, operands):
    return jax.vmap(function)(operands)


def prefill_attention(prefill_query, prefill_key, prefill_value):
    token_rows = prefill_query.shape[0]
    group_size = HEADS // KVH
    score_scale = 1.0 / math.sqrt(HD)
    own_start = lax.axis_index("seq") * token_rows
    query_position = own_start + jnp.arange(token_rows, dtype=jnp.int32)
    query_heads = prefill_query.reshape(token_rows, KVH, group_size, HD)
    initial = (
        jnp.full((KVH, group_size, token_rows), NEGATIVE, jnp.float32),
        jnp.zeros((KVH, group_size, token_rows), jnp.float32),
        jnp.zeros((token_rows, KVH, group_size, HD), jnp.float32),
    )
    key_rows = lax.all_gather(prefill_key, "seq", axis=0, tiled=True)
    value_rows = lax.all_gather(prefill_value, "seq", axis=0, tiled=True)
    key_count = key_rows.shape[0]
    block_rows = 512
    key_heads = key_rows.reshape(key_count, KVH, HD)
    value_heads = value_rows.reshape(key_count, KVH, HD)

    def add_block(number, running_state):
        maxima, totals, weighted = running_state
        offset = number * block_rows
        key_block = lax.dynamic_slice_in_dim(key_heads, offset, block_rows, 0)
        value_block = lax.dynamic_slice_in_dim(value_heads, offset, block_rows, 0)
        key_position = offset + jnp.arange(block_rows, dtype=jnp.int32)
        visible = (key_position[None, :] <= query_position[:, None])[None, None, :, :]
        logits = (
            jnp.einsum("qkgd,pkd->kgqp", query_heads, key_block, preferred_element_type=jnp.float32)
            * score_scale
        )
        logits = jnp.where(visible, logits, NEGATIVE)
        new_maxima = jnp.maximum(maxima, jnp.max(logits, axis=-1))
        exponent = jnp.where(visible, jnp.exp(logits - new_maxima[..., None]), 0.0)
        rescale = jnp.exp(maxima - new_maxima)
        totals = totals * rescale + jnp.sum(exponent, axis=-1)
        weighted = weighted * jnp.moveaxis(rescale, 2, 0)[..., None] + jnp.einsum(
            "kgqp,pkd->qkgd",
            exponent.astype(jnp.bfloat16),
            value_block,
            preferred_element_type=jnp.float32,
        )
        return (new_maxima, totals, weighted)

    maxima, totals, weighted = lax.fori_loop(0, key_count // block_rows, add_block, initial)
    return (
        (weighted / jnp.moveaxis(totals, 2, 0)[..., None])
        .reshape(token_rows, HEADS * HD)
        .astype(jnp.bfloat16)
    )


def decode_attention(dec_query, dec_key_new, dec_value_new, cache_lengths, key_cache, value_cache):
    requests, block_length, feature_width = key_cache.shape
    group_size = HEADS // KVH
    score_scale = 1.0 / math.sqrt(HD)
    first_position = lax.axis_index("seq") * block_length
    positions = first_position + jnp.arange(block_length, dtype=jnp.int32)
    valid_mask = positions[None, :] < cache_lengths[:, None]
    query_heads = dec_query.reshape(requests, KVH, group_size, HD)
    key_heads = key_cache.reshape(requests, block_length, KVH, HD)
    value_heads = value_cache.reshape(requests, block_length, KVH, HD)

    def scores_of(pieces):
        query_one, keys_one, valid_one = pieces
        logits = (
            jnp.einsum("kgd,pkd->kgp", query_one, keys_one, preferred_element_type=jnp.float32)
            * score_scale
        )
        return jnp.where(valid_one[None, None, :], logits, NEGATIVE)

    def terms_of(pieces):
        scores_one, maxima_one, values_one, valid_one = pieces
        exponent = jnp.where(
            valid_one[None, None, :], jnp.exp(scores_one - maxima_one[..., None]), 0.0
        )
        weighted_one = jnp.einsum(
            "kgp,pkd->kgd",
            exponent.astype(jnp.bfloat16),
            values_one,
            preferred_element_type=jnp.float32,
        )
        return (jnp.sum(exponent, axis=-1), weighted_one)

    scores = per_request(scores_of, (query_heads, key_heads, valid_mask))
    local_maxima = jnp.max(scores, axis=-1)
    maxima = lax.pmax(local_maxima, "seq")
    totals, weighted = per_request(terms_of, (scores, maxima, value_heads, valid_mask))
    totals, weighted = lax.psum((totals, weighted), "seq")
    fresh_score = (
        jnp.einsum(
            "rkgd,rkd->rkg",
            query_heads,
            dec_key_new.reshape(requests, KVH, HD),
            preferred_element_type=jnp.float32,
        )
        * score_scale
    )
    final_maxima = jnp.maximum(maxima, fresh_score)
    rescale = jnp.exp(maxima - final_maxima)
    fresh_exp = jnp.exp(fresh_score - final_maxima)
    denominator = totals * rescale + fresh_exp
    fresh_weight = lax.optimization_barrier(fresh_exp.astype(jnp.bfloat16)).astype(jnp.float32)
    numerator = weighted * rescale[..., None] + fresh_weight[..., None] * dec_value_new.reshape(
        requests, KVH, 1, HD
    ).astype(jnp.float32)
    return (numerator / denominator[..., None]).reshape(requests, HEADS * HD).astype(jnp.bfloat16)


def expert_rows(rows_batch, gate_full, up_full, down_full):
    gate_value = jnp.einsum(
        "erd,edf->erf", rows_batch, gate_full, preferred_element_type=jnp.float32
    )
    up_value = jnp.einsum("erd,edf->erf", rows_batch, up_full, preferred_element_type=jnp.float32)
    hidden = (jax.nn.silu(gate_value) * up_value).astype(jnp.bfloat16)
    return jnp.einsum("erf,efd->erd", hidden, down_full, preferred_element_type=jnp.float32).astype(
        jnp.bfloat16
    )


def body(
    prefill_query,
    prefill_key,
    prefill_value,
    prefill_resid,
    dec_query,
    dec_key_new,
    dec_value_new,
    dec_resid,
    cache_lengths,
    key_cache,
    value_cache,
    attn_out_weight,
    ffn_gain,
    expert_gate,
    expert_up,
    expert_down,
    routes,
    route_weights,
):
    attended = prefill_attention(prefill_query, prefill_key, prefill_value)
    middle = (
        prefill_resid.astype(jnp.float32)
        + jnp.dot(attended, attn_out_weight, preferred_element_type=jnp.float32)
    ).astype(jnp.bfloat16)
    normed = rms_scale(middle, ffn_gain)
    gate_full, up_full = (
        lax.all_gather(expert_gate, "req", axis=1, tiled=True),
        lax.all_gather(expert_up, "req", axis=1, tiled=True),
    )
    down_full = lax.all_gather(expert_down, "req", axis=2, tiled=True)
    token_rows, top_count = routes.shape
    flat_expert = routes.reshape(-1)
    token_index = jnp.arange(token_rows * top_count, dtype=jnp.int32) // top_count
    onehot = (flat_expert[:, None] == jnp.arange(EXPERTS, dtype=jnp.int32)[None, :]).astype(
        jnp.int32
    )
    earlier = jnp.cumsum(onehot, axis=0) - onehot
    slot_index = jnp.sum(earlier * onehot, axis=1)
    outgoing = (
        jnp.zeros((EXPERTS, CAP, D), jnp.bfloat16)
        .at[flat_expert, slot_index]
        .set(normed[token_index])
    )
    incoming = lax.all_to_all(outgoing[:, None], "seq", split_axis=0, concat_axis=1, tiled=True)
    local_experts, sources, slot_count, feature_width = incoming.shape
    result = expert_rows(
        incoming.reshape(local_experts, sources * slot_count, feature_width),
        gate_full,
        up_full,
        down_full,
    )
    result = result.reshape(local_experts, sources, slot_count, feature_width)
    returned = lax.all_to_all(result, "seq", split_axis=1, concat_axis=0, tiled=True)
    picked = returned.reshape(EXPERTS, CAP, D)[flat_expert, slot_index]
    picked = picked.reshape(token_rows, top_count, D)
    mixture = jnp.sum(route_weights[..., None] * picked.astype(jnp.float32), axis=1)
    prefill_out = (middle.astype(jnp.float32) + mixture).astype(jnp.bfloat16)
    decoded = decode_attention(
        dec_query, dec_key_new, dec_value_new, cache_lengths, key_cache, value_cache
    )
    dec_out = (
        dec_resid.astype(jnp.float32)
        + jnp.dot(decoded, attn_out_weight, preferred_element_type=jnp.float32)
    ).astype(jnp.bfloat16)
    return (prefill_out, dec_out)


def solution(mesh):
    return jax.shard_map(
        body,
        mesh=mesh,
        in_specs=(
            P(("req", "seq"), None),
            P(("req", "seq"), None),
            P(("req", "seq"), None),
            P(("req", "seq"), None),
            P("req", None),
            P("req", None),
            P("req", None),
            P("req", None),
            P("req"),
            P("req", "seq", None),
            P("req", "seq", None),
            P(),
            P(),
            P("seq", "req", None),
            P("seq", "req", None),
            P("seq", None, "req"),
            P(("req", "seq"), None),
            P(("req", "seq"), None),
        ),
        out_specs=(P(("req", "seq"), None), P("req", None)),
        check_vma=False,
    )
```

profile of v0, /device:TPU:0, one launch (start us, length us, event | category | flops | bytes accessed | tf_op | source)
XLA Modules:
  0.0 821.3 jit_solution(3442623777327935929)
XLA Ops:
  11.1 1.2 copy.41
  12.3 9.0 %reduce-window.6 = s32[32,8,128]{2,1,0:T(8,128)S(1)} reduce-window(s32[32,8,128]{2,1,0:T(8,128)S(1)} %fusion.51, s32[]{:T(128)} %constant.93.clone.1), window={size=1x1x128 pad=0_0x0_0x127_0}, to_apply=%region_4.5 | reduce-window | flops 4161536 | bytes 262148 | tf_op jit(solution)/shard_map/reduce-window
  23.4 72.7 %all-gather.6.cloned.1.call-done = bf16[4096,512]{1,0:T(8,128)(2,1)} async-done(((bf16[128,512]{1,0:T(8,128)(2,1)}), bf16[4096,512]{1,0:T(8,128)(2,1)}) %all-gather.6.cloned.1.call-update) | async-done | bytes 4194320 | tf_op jit(solution)/shard_map/all_gather | solution.py:39
  96.1 6.4 copy.40
  102.5 75.9 %all-gather.8.cloned.1.call-done = bf16[4096,512]{1,0:T(8,128)(2,1)} async-done(((bf16[128,512]{1,0:T(8,128)(2,1)}), bf16[4096,512]{1,0:T(8,128)(2,1)}) %all-gather.8.cloned.1.call-update) | async-done | bytes 4194320 | tf_op jit(solution)/shard_map/all_gather | solution.py:40
  178.4 6.4 copy.42
  184.8 98.8 %while.18 = (s32[]{:T(128)}, f32[8,3,128]{2,1,0:T(4,128)S(1)}, f32[8,3,128]{2,1,0:T(4,128)S(1)}, f32[128,8,3,64]{0,3,2,1:T(8,128)S(1)}, bf16[4096,8,64]{0,2,1:T(...) while((s32[]{:T(128)}, f32[8,3,128]{2,1,0:T(4,128)S(1)}, ...), condition=%wide.region_3.4_spmd.clone, body=%wide.region_0.3_spmd.clone.sunk | while | flops 423774848 | bytes 47518944 | solution.py:70
  185.0 4.8 fusion.83
  189.8 4.5 fusion.85
  194.5 2.8 fusion.87
  197.5 4.8 fusion.83
  202.3 4.4 fusion.85
  206.9 2.8 fusion.87
  209.8 4.8 fusion.83
  214.6 4.4 fusion.85
  219.2 2.8 fusion.87
  222.2 4.8 fusion.83
  227.0 4.4 fusion.85
  231.6 2.8 fusion.87
  234.5 4.8 fusion.83
  239.3 4.4 fusion.85
  243.9 2.8 fusion.87
  246.8 4.8 fusion.83
  251.6 4.4 fusion.85
  256.2 2.8 fusion.87
  259.2 4.8 fusion.83
  263.9 4.4 fusion.85
  268.5 2.8 fusion.87
  271.5 4.8 fusion.83
  276.3 4.4 fusion.85
  280.8 2.8 fusion.87
  283.7 3.2 multiply_reduce_fusion
  287.0 0.9 copy-done.1
  288.0 18.6 %scatter_custom_fusion = bf16[1280,1536]{1,0:T(8,128)(2,1)} fusion(s32[1024]{0:T(1024)S(1)} %get-tuple-element.207, bf16[128,1536]{1,0:T(8,128)(2,1)S(1)} %multiply_convert_fusion, s32[1024]{0:T(1024)S(1)} %get-tuple-element.206, bf16[]{:T(256)} %constant.98.clone.1), kind=kCustom, calls=%fused_computation.36 | custom fusion | bytes 3932162
  306.7 5.1 all-to-all-start
  312.4 52.8 %all-to-all-done = bf16[32,1,40,1536]{3,2,1,0:T(8,128)(2,1)} async-done(((bf16[32,1,40,1536]{3,2,1,0:T(8,128)(2,1)}), bf16[32,1,40,1536]{3,2,1,0:T(8,128)(2,1)}, u32[]{:S(2)}, u32[]{:S(2)}) %all-to-all-start) | async-done | bytes 3932192 | tf_op jit(solution)/shard_map/all_to_all | solution.py:190
  365.2 4.8 fusion.36
  370.1 9.5 %convolution_convert_fusion = bf16[1280,1536]{1,0:T(8,128)(2,1)} fusion(bf16[1,512,1536]{2,1,0:T(8,128)(2,1)} %all-gather.14.cloned.1.call-done, bf16[1280,1536]{1,0:T(8,128)(2,1)} %bitcast.10, f32[1280,512]{1,0:T(8,128)S(1)} %fusion.36, bf16[1,1536,512]{2,1,0:T(8,128)(2,1)} %all-gather.12.cloned.1.call-done), kind=kOutput, calls=%fused_computation.32 | convolution fusion | flops 4032430080 | bytes 13631488 | tf_op jit(solution)/shard_map/erf,efd->erd/dot_general | solution.py:141
  379.5 7.5 all-to-all-start.1
  387.2 6.3 copy.51
  393.7 6.3 copy.50
  400.2 2.9 fusion.58
  403.2 205.7 %pmax.7 = f32[4,8,3]{2,1,0:T(8,128)S(1)} all-reduce(f32[4,8,3]{2,1,0:T(8,128)S(1)} %get-tuple-element.204), channel_id=1, replica_groups=mesh['req'=4,'seq'=32] {'seq'}, use_global_device_ids=true, to_apply=%region_11.12 | all-reduce | flops 96 | bytes 768 | tf_op jit(solution)/shard_map/pmax | solution.py:112
  609.3 3.5 fusion.43
  612.7 176.5 %all-reduce = (f32[4,8,3,64]{3,2,1,0:T(4,128)S(1)}, f32[4,8,3]{2,1,0:T(8,128)S(1)}) all-reduce(f32[4,8,3,64]{3,2,1,0:T(4,128)S(1)} %fusion.43, f32[4,8,3]{2,1,0:T(8,128)S(1)} %fusion.41), channel_id=1, replica_groups=mesh['req'=4,'seq'=32] {'seq'}, use_global_device_ids=true, to_apply=%region_12.13 | all-reduce | flops 6240 | bytes 49920 | tf_op jit(solution)/shard_map/psum | solution.py:114
  789.7 3.7 fusion.32
  793.4 17.8 %gather_fusion = bf16[1024,1536]{1,0:T(8,128)(2,1)S(1)} fusion(bf16[32,40,1536]{2,1,0:T(8,128)(2,1)} %bitcast.16, s32[1024]{0:T(1024)S(1)} %bitcast.111), kind=kCustom, calls=%fused_computation.1 | custom fusion | bytes 6299648 | tf_op jit(solution)/shard_map/gather | solution.py:200
  811.2 2.8 fusion.26
  (133 shorter events, 11.4 us)
Async XLA Ops:
  7.2 88.9 %all-gather.6.cloned.1.call-start = ((), (), s32[]{:S(2)}) async-start(), calls=%async_computation.2 | async-start | bytes 4325376 | tf_op jit(solution)/shard_map/all_gather | solution.py:39
  7.9 170.5 %all-gather.8.cloned.1.call-start = ((), (), s32[]{:S(2)}) async-start(), calls=%async_computation.3 | async-start | bytes 4325376 | tf_op jit(solution)/shard_map/all_gather | solution.py:40
  8.6 303.7 %all-gather.10.cloned.1.call-start = ((), (), s32[]{:S(2)}) async-start(), calls=%async_computation.4 | async-start | bytes 1966080 | tf_op jit(solution)/shard_map/all_gather | solution.py:173
  9.4 360.7 %all-gather.14.cloned.1.call-start = ((), (), s32[]{:S(2)}) async-start(), calls=%async_computation.6 | async-start | bytes 1966080 | tf_op jit(solution)/shard_map/all_gather | solution.py:176
  184.8 98.9 %copy-start.3 = (bf16[128,1536]{1,0:T(8,128)(2,1)S(1)}, bf16[128,1536]{1,0:T(8,128)(2,1)}, u32[]{:S(2)}) copy-start(bf16[128,1536]{1,0:T(8,128)(2,1)} %param.23) | copy-start | bytes 1179652
  189.8 4.7 copy-start
  202.3 4.6 copy-start
  214.6 4.6 copy-start
  227.0 4.6 copy-start
  239.3 4.6 copy-start
  251.6 4.6 copy-start
  263.9 4.6 copy-start
  276.2 4.6 copy-start
  283.6 4.3 copy-start.6
  287.0 0.9 copy-start.1
  306.7 58.5 %all-to-all-start = ((bf16[32,1,40,1536]{3,2,1,0:T(8,128)(2,1)}), bf16[32,1,40,1536]{3,2,1,0:T(8,128)(2,1)}, u32[]{:S(2)}, u32[]{:S(2)}) async-start(bf16[32,1,40,1536]{3,2,1,0:T(8,128)(2,1)} %bitcast.114), calls=%async_computation | async-start | bytes 7864320 | tf_op jit(solution)/shard_map/all_to_all | solution.py:190
  311.8 58.3 %all-gather.12.cloned.1.call-start = ((), (), s32[]{:S(2)}) async-start(), calls=%async_computation.5 | async-start | bytes 1966080 | tf_op jit(solution)/shard_map/all_gather | solution.py:174
  379.5 7.6 copy-start.7
  379.5 413.8 %all-to-all-start.1 = ((bf16[1,32,40,1536]{3,2,0,1:T(8,128)(2,1)}), bf16[1,32,40,1536]{3,2,0,1:T(8,128)(2,1)}, u32[]{:S(2)}, u32[]{:S(2)}) async-start(bf16[1,32,40,1536]{3,2,0,1:T(8,128)(2,1)} %bitcast.118), calls=%async_computation.1 | async-start | bytes 7864320 | tf_op jit(solution)/shard_map/all_to_all | solution.py:199
  387.2 6.3 copy-start.4
  393.6 6.4 copy-start.8
  393.6 6.4 copy-start.9
  393.7 6.5 copy-start.10
  403.2 386.5 %copy-start.5 = (bf16[4,1536]{1,0:T(4,128)(2,1)S(1)}, bf16[4,1536]{1,0:T(4,128)(2,1)}, u32[]{:S(2)}) copy-start(bf16[4,1536]{1,0:T(4,128)(2,1)} %param.27) | copy-start | bytes 36868
  811.2 2.8 copy-start.2
Sparse Core Ops, SparseCore 0:
  11.0 85.0 all-gather.5
  99.1 79.3 all-gather.7
  180.1 21.5 all-gather.9
  203.2 25.7 all-gather.13
  313.9 54.2 all-gather.11
where the time goes:
time: 823 us; the launch traced here: 821 us
  blocking collectives  382 us (46%)
  waiting for transfers between devices  204 us (25%)
  matrix products  88 us (11%)
  local copies, waits for them, and re-layouts  67 us (8%)
  other arithmetic  52 us (6%)
  between operations  14.1 us (2%)
  starting transfers between devices  13 us (2%)
    pmax x1, blocking collectives, decode_attention(): maxima = lax.pmax(local_maxima, 'seq')  206 us
    psum x1, blocking collectives, decode_attention(): totals, weighted = lax.psum((totals, weighted), 'seq')  176 us
    all_gather x1, waiting for transfers between devices, prefill_attention(): value_rows = lax.all_gather(prefill_value, 'seq', axis=0, tiled=True)  75.9 us
    all_gather x1, waiting for transfers between devices, prefill_attention(): key_rows = lax.all_gather(prefill_key, 'seq', axis=0, tiled=True)  72.7 us
    all_to_all x1, waiting for transfers between devices, body(): lax.all_to_all(outgoing[:, None], 'seq', split_axis=0, concat_axis=1, til...  52.8 us
    dot_general x8, matrix products, add_block(): jnp.einsum('qkgd,pkd->kgqp', query_heads, key_block, preferred_element_ty...  38.2 us
    reduce_sum x8, other arithmetic, add_block(): totals = totals * rescale + jnp.sum(exponent, axis=-1)  35.4 us
    unnamed x26, local copies, waits for them, and re-layouts  34.3 us
  transfers between devices with their start and end apart: 7, of which 3 were waited for; matrix products, arithmetic and copies ran while one was open for 21% of the time, Pallas kernels for 0%

commit v1 on v0

--- a/solution.py
+++ b/solution.py
@@ -37,7 +37,10 @@
         jnp.zeros((token_rows, KVH, group_size, HD), jnp.float32),
     )
     key_rows = lax.all_gather(prefill_key, "seq", axis=0, tiled=True)
-    value_rows = lax.all_gather(prefill_value, "seq", axis=0, tiled=True)
+    count = lax.axis_size("seq")
+    parts = jnp.stack([prefill_value for _ in range(count)])
+    parts = lax.all_to_all(parts, "seq", split_axis=0, concat_axis=0)
+    value_rows = jnp.concatenate(parts, axis=0)
     key_count = key_rows.shape[0]
     block_rows = 512
     key_heads = key_rows.reshape(key_count, KVH, HD)

time: 823 us -> 780 us (0.948)
  waiting for transfers between devices: 204 us -> 139 us
  starting transfers between devices: 13 us -> 24 us
  local copies, waits for them, and re-layouts: 67 us -> 76.9 us
    all_gather x1 -> x0, waiting for transfers between devices: 75.9 us -> none  [prefill_attention(): value_rows = lax.all_gather(prefill_value, 'seq', axis=0, tiled=True)]
    all_to_all x0 -> x1, waiting for transfers between devices: none -> 48.9 us  [prefill_attention(): parts = lax.all_to_all(parts, 'seq', split_axis=0, concat_axis=0)]
    all_gather x1, waiting for transfers between devices: 72.7 us -> 34.9 us  [prefill_attention(): key_rows = lax.all_gather(prefill_key, 'seq', axis=0, tiled=True)]
    all_to_all x0 -> x1, starting transfers between devices: none -> 11 us  [prefill_attention(): parts = lax.all_to_all(parts, 'seq', split_axis=0, concat_axis=0)]
    another operation x2 -> x4, local copies, waits for them, and re-layouts: 0.08 us -> 10.3 us  [the longest x1 7.32 us: prefill_attention(): value_heads = value_rows.reshape(key_count, KVH, HD)]
    unnamed x26 -> x35, local copies, waits for them, and re-layouts: 34.3 us -> 33.7 us
  transfers between devices with their start and end apart: 7 -> 7, of which waited for: 3 -> 3; matrix products, arithmetic and copies ran while one was open for 21% -> 24% of each run, Pallas kernels for 0% -> 0%
where the time goes in v1:
time: 780 us; the launch traced here: 778 us
  blocking collectives  383 us (49%)
  waiting for transfers between devices  139 us (18%)
  matrix products  88.6 us (11%)
  local copies, waits for them, and re-layouts  76.9 us (10%)
  other arithmetic  51.1 us (7%)
  starting transfers between devices  24 us (3%)
  between operations  14.1 us (2%)
    pmax x1, blocking collectives, decode_attention(): maxima = lax.pmax(local_maxima, 'seq')  207 us
    psum x1, blocking collectives, decode_attention(): totals, weighted = lax.psum((totals, weighted), 'seq')  176 us
    all_to_all x1, waiting for transfers between devices, body(): lax.all_to_all(outgoing[:, None], 'seq', split_axis=0, concat_axis=1, til...  52.8 us
    all_to_all x1, waiting for transfers between devices, prefill_attention(): parts = lax.all_to_all(parts, 'seq', split_axis=0, concat_axis=0)  48.9 us
    dot_general x8, matrix products, add_block(): jnp.einsum('qkgd,pkd->kgqp', query_heads, key_block, preferred_element_ty...  38 us
    reduce_sum x8, other arithmetic, add_block(): totals = totals * rescale + jnp.sum(exponent, axis=-1)  35.6 us
    all_gather x1, waiting for transfers between devices, prefill_attention(): key_rows = lax.all_gather(prefill_key, 'seq', axis=0, tiled=True)  34.9 us
    unnamed x35, local copies, waits for them, and re-layouts  33.7 us
  transfers between devices with their start and end apart: 7, of which 3 were waited for; matrix products, arithmetic and copies ran while one was open for 24% of the time, Pallas kernels for 0%

profile of v1, /device:TPU:0, one launch (start us, length us, event | category | flops | bytes accessed | tf_op | source)
XLA Modules:
  0.0 777.6 jit_solution(10528343287864051817)
XLA Ops:
  8.9 2.9 stack.2
  11.8 11.0 %all-to-all-start = ((bf16[32,128,512]{1,2,0:T(8,128)(2,1)}), bf16[32,128,512]{1,2,0:T(8,128)(2,1)}, u32[]{:S(2)}, u32[]{:S(2)}) async-start(bf16[32,128,512]{1,2,0:T(8,128)(2,1)} %stack.2), calls=%async_computation | async-start | bytes 8388608 | tf_op jit(solution)/shard_map/all_to_all | solution.py:42
  25.0 9.0 %reduce-window.6 = s32[32,8,128]{2,1,0:T(8,128)S(1)} reduce-window(s32[32,8,128]{2,1,0:T(8,128)S(1)} %fusion.51, s32[]{:T(128)} %constant.93.clone.1), window={size=1x1x128 pad=0_0x0_0x127_0}, to_apply=%region_4.5 | reduce-window | flops 4161536 | bytes 262148 | tf_op jit(solution)/shard_map/reduce-window
  34.8 48.9 %all-to-all-done = bf16[32,128,512]{1,2,0:T(8,128)(2,1)} async-done(((bf16[32,128,512]{1,2,0:T(8,128)(2,1)}), bf16[32,128,512]{1,2,0:T(8,128)(2,1)}, u32[]{:S(2)}, u32[]{:S(2)}) %all-to-all-start) | async-done | bytes 4194336 | tf_op jit(solution)/shard_map/all_to_all | solution.py:42
  83.7 7.0 copy.56
  90.7 7.3 reshape_reshape.3
  98.0 34.9 %all-gather.5.cloned.1.call-done = bf16[4096,512]{1,0:T(8,128)(2,1)} async-done(((bf16[128,512]{1,0:T(8,128)(2,1)}), bf16[4096,512]{1,0:T(8,128)(2,1)}) %all-gather.5.cloned.1.call-update) | async-done | bytes 4194320 | tf_op jit(solution)/shard_map/all_gather | solution.py:39
  132.9 6.4 copy.53
  139.3 99.5 %while.18 = (s32[]{:T(128)}, f32[8,3,128]{2,1,0:T(4,128)S(1)}, f32[8,3,128]{2,1,0:T(4,128)S(1)}, f32[128,8,3,64]{0,3,2,1:T(8,128)S(1)}, bf16[4096,8,64]{0,2,1:T(...) while((s32[]{:T(128)}, f32[8,3,128]{2,1,0:T(4,128)S(1)}, ...), condition=%wide.region_3.4_spmd.clone, body=%wide.region_0.3_spmd.clone.sunk | while | flops 423774848 | bytes 47518944 | solution.py:73
  139.5 4.8 fusion.83
  144.3 4.5 fusion.85
  149.0 2.9 fusion.87
  152.0 4.8 fusion.83
  156.8 4.4 fusion.85
  161.4 2.9 fusion.87
  164.5 4.7 fusion.83
  169.2 4.4 fusion.85
  173.9 2.9 fusion.87
  176.9 4.8 fusion.83
  181.7 4.4 fusion.85
  186.3 2.9 fusion.87
  189.3 4.7 fusion.83
  194.1 4.4 fusion.85
  198.7 2.9 fusion.87
  201.8 4.7 fusion.83
  206.5 4.4 fusion.85
  211.1 2.9 fusion.87
  214.2 4.7 fusion.83
  218.9 4.4 fusion.85
  223.5 2.9 fusion.87
  226.6 4.7 fusion.83
  231.3 4.4 fusion.85
  235.9 2.9 fusion.87
  238.9 3.2 multiply_reduce_fusion
  243.2 18.6 %scatter_custom_fusion = bf16[1280,1536]{1,0:T(8,128)(2,1)} fusion(s32[1024]{0:T(1024)S(1)} %get-tuple-element.207, bf16[128,1536]{1,0:T(8,128)(2,1)S(1)} %multiply_convert_fusion, s32[1024]{0:T(1024)S(1)} %get-tuple-element.206, bf16[]{:T(256)} %constant.98.clone.1), kind=kCustom, calls=%fused_computation.36 | custom fusion | bytes 3932162
  261.9 5.1 all-to-all-start.1
  267.6 52.8 %all-to-all-done.1 = bf16[32,1,40,1536]{3,2,1,0:T(8,128)(2,1)} async-done(((bf16[32,1,40,1536]{3,2,1,0:T(8,128)(2,1)}), bf16[32,1,40,1536]{3,2,1,0:T(8,128)(2,1)}, u32[]{:S(2)}, u32[]{:S(2)}) %all-to-all-start.1) | async-done | bytes 3932192 | tf_op jit(solution)/shard_map/all_to_all | solution.py:193
  320.4 4.8 fusion.36
  325.3 9.4 %convolution_convert_fusion = bf16[1280,1536]{1,0:T(8,128)(2,1)} fusion(bf16[1,512,1536]{2,1,0:T(8,128)(2,1)} %all-gather.11.cloned.1.call-done, bf16[1280,1536]{1,0:T(8,128)(2,1)} %bitcast.9, f32[1280,512]{1,0:T(8,128)S(1)} %fusion.36, bf16[1,1536,512]{2,1,0:T(8,128)(2,1)} %all-gather.9.cloned.1.call-done), kind=kOutput, calls=%fused_computation.32 | convolution fusion | flops 4032430080 | bytes 13631488 | tf_op jit(solution)/shard_map/erf,efd->erd/dot_general | solution.py:144
  334.7 7.5 all-to-all-start.2
  342.4 6.3 copy.65
  348.8 6.3 copy.64
  355.4 2.9 fusion.58
  358.3 206.8 %pmax.7 = f32[4,8,3]{2,1,0:T(8,128)S(1)} all-reduce(f32[4,8,3]{2,1,0:T(8,128)S(1)} %get-tuple-element.204), channel_id=1, replica_groups=mesh['req'=4,'seq'=32] {'seq'}, use_global_device_ids=true, to_apply=%region_11.12 | all-reduce | flops 96 | bytes 768 | tf_op jit(solution)/shard_map/pmax | solution.py:115
  565.5 3.4 fusion.43
  568.9 176.5 %all-reduce = (f32[4,8,3,64]{3,2,1,0:T(4,128)S(1)}, f32[4,8,3]{2,1,0:T(8,128)S(1)}) all-reduce(f32[4,8,3,64]{3,2,1,0:T(4,128)S(1)} %fusion.43, f32[4,8,3]{2,1,0:T(8,128)S(1)} %fusion.41), channel_id=1, replica_groups=mesh['req'=4,'seq'=32] {'seq'}, use_global_device_ids=true, to_apply=%region_12.13 | all-reduce | flops 6240 | bytes 49920 | tf_op jit(solution)/shard_map/psum | solution.py:117
  745.9 3.7 fusion.32
  749.6 17.8 %gather_fusion = bf16[1024,1536]{1,0:T(8,128)(2,1)S(1)} fusion(bf16[32,40,1536]{2,1,0:T(8,128)(2,1)} %bitcast.15, s32[1024]{0:T(1024)S(1)} %bitcast.112), kind=kCustom, calls=%fused_computation.1 | custom fusion | bytes 6299648 | tf_op jit(solution)/shard_map/gather | solution.py:203
  (143 shorter events, 13.6 us)
Async XLA Ops:
  7.2 125.7 %all-gather.5.cloned.1.call-start = ((), (), s32[]{:S(2)}) async-start(), calls=%async_computation.3 | async-start | bytes 4325376 | tf_op jit(solution)/shard_map/all_gather | solution.py:39
  11.8 12.5 %copy-start.8 = (s32[128,8]{0,1:T(8,128)S(1)}, s32[128,8]{0,1:T(8,128)}, u32[]{:S(2)}) copy-start(s32[128,8]{0,1:T(8,128)} %param.36) | copy-start | bytes 12292
  11.8 12.9 %copy-start.4 = (bf16[128,1536]{1,0:T(8,128)(2,1)S(1)}, bf16[128,1536]{1,0:T(8,128)(2,1)}, u32[]{:S(2)}) copy-start(bf16[128,1536]{1,0:T(8,128)(2,1)} %param.20) | copy-start | bytes 1179652
  11.8 22.8 %copy-start.14 = (s32[2]{0:T(128)S(1)}, s32[2]{0:T(128)}, u32[]{:S(2)}) copy-start(s32[2]{0:T(128)} %constant.114) | copy-start | bytes 28
  11.8 22.8 %copy-start.13 = (s32[2]{0:T(128)S(1)}, s32[2]{0:T(128)}, u32[]{:S(2)}) copy-start(s32[2]{0:T(128)} %constant.117) | copy-start | bytes 28
  11.8 71.9 %all-to-all-start = ((bf16[32,128,512]{1,2,0:T(8,128)(2,1)}), bf16[32,128,512]{1,2,0:T(8,128)(2,1)}, u32[]{:S(2)}, u32[]{:S(2)}) async-start(bf16[32,128,512]{1,2,0:T(8,128)(2,1)} %stack.2), calls=%async_computation | async-start | bytes 8388608 | tf_op jit(solution)/shard_map/all_to_all | solution.py:42
  22.8 244.7 %all-gather.7.cloned.1.call-start = ((), (), s32[]{:S(2)}) async-start(), calls=%async_computation.4 | async-start | bytes 1966080 | tf_op jit(solution)/shard_map/all_gather | solution.py:176
  23.6 301.7 %all-gather.11.cloned.1.call-start = ((), (), s32[]{:S(2)}) async-start(), calls=%async_computation.6 | async-start | bytes 1966080 | tf_op jit(solution)/shard_map/all_gather | solution.py:179
  139.3 99.6 %copy-start.3 = (bf16[128,1536]{1,0:T(8,128)(2,1)S(1)}, bf16[128,1536]{1,0:T(8,128)(2,1)}, u32[]{:S(2)}) copy-start(bf16[128,1536]{1,0:T(8,128)(2,1)} %param.23) | copy-start | bytes 1179652
  144.3 4.7 copy-start
  156.8 4.6 copy-start
  169.2 4.6 copy-start
  181.7 4.6 copy-start
  194.1 4.6 copy-start
  206.5 4.6 copy-start
  218.9 4.6 copy-start
  231.3 4.6 copy-start
  238.8 4.3 copy-start.7
  242.2 0.9 copy-start.1
  261.9 58.6 %all-to-all-start.1 = ((bf16[32,1,40,1536]{3,2,1,0:T(8,128)(2,1)}), bf16[32,1,40,1536]{3,2,1,0:T(8,128)(2,1)}, u32[]{:S(2)}, u32[]{:S(2)}) async-start(bf16[32,1,40,1536]{3,2,1,0:T(8,128)(2,1)} %bitcast.115), calls=%async_computation.1 | async-start | bytes 7864320 | tf_op jit(solution)/shard_map/all_to_all | solution.py:193
  267.0 58.3 %all-gather.9.cloned.1.call-start = ((), (), s32[]{:S(2)}) async-start(), calls=%async_computation.5 | async-start | bytes 1966080 | tf_op jit(solution)/shard_map/all_gather | solution.py:177
  334.7 7.6 copy-start.9
  334.7 414.9 %all-to-all-start.2 = ((bf16[1,32,40,1536]{3,2,0,1:T(8,128)(2,1)}), bf16[1,32,40,1536]{3,2,0,1:T(8,128)(2,1)}, u32[]{:S(2)}, u32[]{:S(2)}) async-start(bf16[1,32,40,1536]{3,2,0,1:T(8,128)(2,1)} %bitcast.118), calls=%async_computation.2 | async-start | bytes 7864320 | tf_op jit(solution)/shard_map/all_to_all | solution.py:202
  342.3 6.3 copy-start.5
  348.8 6.4 copy-start.10
  348.8 6.5 copy-start.11
  348.8 6.5 copy-start.12
  358.3 387.6 %copy-start.6 = (bf16[4,1536]{1,0:T(4,128)(2,1)S(1)}, bf16[4,1536]{1,0:T(4,128)(2,1)}, u32[]{:S(2)}) copy-start(bf16[4,1536]{1,0:T(4,128)(2,1)} %param.27) | copy-start | bytes 36868
  767.4 2.9 copy-start.2
Sparse Core Ops, SparseCore 0:
  11.0 121.8 all-gather.4
  134.6 21.5 all-gather.6
  157.8 25.7 all-gather.10
  269.2 54.1 all-gather.8
